TPU v7x, 32 devices: a whole 2x2x4 slice. The times are simulated.
32 devices in a mesh: wide: 8 (over z, y), narrow: 4 (over x, core).
Axes of the slice: x: 2, y: 2, z: 4, core: 2. Of those that a mesh axis runs over, the one named last changes fastest.
Arguments:
- residual: float32 [8, 4, 6, 192, 512], P('wide', 'narrow'), may hold values from -6 to 6
- face_schur: float32 [8, 4, 6, 192, 192], P('wide', 'narrow'), may hold values from -0.5 to 1.5, as said below
- local_solver: bfloat16 [8, 4, 1152, 1152], P('wide', 'narrow'), may hold values from -0.1875 to 0.1875
- interface_functional_set: float32 [3, 192, 16], replicated, may hold values from -0.4375 to 0.4375
- coarse_inverse: float32 [1536, 1536], P('wide', 'narrow'), may hold values from -0.3125 to 0.3125
Outputs:
- preconditioned: float32 [8, 4, 3, 192, 512], P('wide', 'narrow')
Inputs may be any that keep to these rules, and one draw needn't show every extreme that they name: `face_schur`: every face block is symmetric positive definite.
All inputs are finite; a program needn't handle non-finite values. Where the computation divides by a largest or mean magnitude, that divisor is 1e-20 or more.
Results may differ from a plain program's by a relative error of at most 0.002.
Values sent between devices are 32-bit elements; how exact they have to be, the bound alone decides.
No kernel may reach another device: no remote copies, remote signals or barrier semaphores. Data moves between devices by JAX's collectives and lax.ppermute only.
A program may use at most 64 MiB of HBM per device.

v0:
```python
import jax
import jax.numpy as jnp
from jax import lax
from jax.sharding import PartitionSpec as P

NS_STEPS = 12
exact_arithmetic_mode = lax.Precision.HIGHEST


def passed_along(value, axis, steps):
    count = lax.axis_size(axis)
    pairs = [(source, (source + steps) % count) for source in range(count)]
    return lax.ppermute(value, axis, pairs)


def newton_schulz(matrices):
    row_sums = jnp.max(jnp.sum(jnp.abs(matrices), axis=2), axis=1)
    approx = matrices / (row_sums * row_sums)[:, None, None]
    for iteration in range(NS_STEPS):
        product = jnp.einsum("bij,bjk->bik", matrices, approx, precision=exact_arithmetic_mode)
        approx = 2.0 * approx - jnp.einsum(
            "bij,bjk->bik", approx, product, precision=exact_arithmetic_mode
        )
    return approx


def apply_faces(blocks, fields):
    return jnp.einsum("fij,fjr->fir", blocks, fields, precision=exact_arithmetic_mode)


def per_device(residual, face_schur, local_solver, interface_functional_set, coarse_inverse):
    blocks = face_schur[0, 0]
    face_loads = residual[0, 0]
    face_order = blocks.shape[1]
    columns_count = face_loads.shape[2]
    wide_low = jnp.concatenate([blocks[0], face_loads[0]], axis=1)
    wide_above = passed_along(wide_low, "wide", -1)
    narrow_low = jnp.concatenate([blocks[2], face_loads[2]], axis=1)
    narrow_above = passed_along(narrow_low, "narrow", -1)
    owned_sums = jnp.stack(
        [
            blocks[1] + wide_above[:, :face_order],
            blocks[3] + narrow_above[:, :face_order],
            blocks[4] + blocks[5],
        ],
        axis=0,
    )
    owned_values = jnp.stack(
        [
            face_loads[1] + wide_above[:, face_order:],
            face_loads[3] + narrow_above[:, face_order:],
            face_loads[4] + face_loads[5],
        ],
        axis=0,
    )
    owned_inverse = newton_schulz(owned_sums)
    owned_scaled = apply_faces(owned_inverse, owned_values)
    wide_below = passed_along(owned_scaled[0], "wide", 1)
    narrow_below = passed_along(owned_scaled[1], "narrow", 1)
    face_scaled = jnp.stack(
        [
            wide_below,
            owned_scaled[0],
            narrow_below,
            owned_scaled[1],
            owned_scaled[2],
            owned_scaled[2],
        ],
        axis=0,
    )
    restricted_residual = jnp.einsum(
        "psk,pse->pke", interface_functional_set, owned_values, precision=exact_arithmetic_mode
    )
    restricted_residual = restricted_residual.reshape(-1, columns_count)
    incomplete_total = jnp.dot(
        coarse_inverse,
        lax.all_gather(restricted_residual, "wide", axis=0, tiled=True),
        precision=exact_arithmetic_mode,
        preferred_element_type=jnp.float32,
    )
    own_rows = restricted_residual.shape[0]
    summed = lax.psum(incomplete_total, "narrow")
    own_coarse = lax.dynamic_slice_in_dim(summed, lax.axis_index("narrow") * own_rows, own_rows, 0)
    local_loads = apply_faces(blocks, face_scaled).astype(jnp.bfloat16)
    flattened = local_loads.reshape(-1, columns_count)
    solved = jnp.dot(local_solver[0, 0], flattened, preferred_element_type=jnp.float32)
    solved = solved.reshape(6, face_order, columns_count)
    weighted = apply_faces(blocks, solved)
    wide_back = passed_along(weighted[0], "wide", -1)
    narrow_back = passed_along(weighted[2], "narrow", -1)
    combined = jnp.stack(
        [weighted[1] + wide_back, weighted[3] + narrow_back, weighted[4] + weighted[5]], axis=0
    )
    local_part = apply_faces(owned_inverse, combined)
    update_increment = own_coarse.reshape(3, -1, columns_count)
    coarse_component = jnp.einsum(
        "fek,fkg->feg", interface_functional_set, update_increment, precision=exact_arithmetic_mode
    )
    output_answer = local_part + coarse_component
    return output_answer[None, None]


def solution(mesh):
    placed = (
        P("wide", "narrow", None, None, None),
        P("wide", "narrow", None, None, None),
        P("wide", "narrow", None, None),
        P(),
        P("wide", "narrow"),
    )
    return jax.shard_map(
        per_device,
        mesh=mesh,
        in_specs=placed,
        out_specs=P("wide", "narrow", None, None, None),
        check_vma=False,
    )
```

profile of v0, /device:TPU:0, one launch (start us, length us, event | category | flops | bytes accessed | tf_op | source)
XLA Modules:
  0.0 147.2 jit_solution(12711466252790806071)
XLA Ops:
  6.5 1.4 add_bitcast_fusion.1
  8.0 2.3 %slice_bitcast_fusion.6 = (f32[192,512]{1,0:T(8,128)S(1)}, f32[192,512]{1,0:T(8,128)S(1)}, f32[1,192,512]{2,1,0:T(8,128)}) fusion(f32[1,1,6,192,512]{4,3,2,1,0:T(8,128)} %param.5), kind=kLoop, calls=%fused_computation.57 | loop fusion | flops 98304 | bytes 2752512 | tf_op jit(solution)/shard_map/squeeze | solution.py:36
  10.4 2.5 %collective-permute-start.1 = (f32[192,704]{1,0:T(8,128)S(1)}, f32[192,704]{1,0:T(8,128)S(1)}, u32[]{:S(2)}, u32[]{:S(2)}) collective-permute-start(f32[192,704]{1,0:T(8,128)S(1)} %pad_maximum_fusion.4), channel_id=1, source_target_pairs={{0,3},{1,0},{2,1},{3,2},{4,7},{5,4},{6,5},{7,6},{8,11},{9,8},{10,9... | collective-permute-start | bytes 1622024 | tf_op jit(solution)/shard_map/ppermute | solution.py:13
  13.1 4.6 %collective-permute-start = (f32[192,704]{1,0:T(8,128)S(1)}, f32[192,704]{1,0:T(8,128)S(1)}, u32[]{:S(2)}, u32[]{:S(2)}) collective-permute-start(f32[192,704]{1,0:T(8,128)S(1)} %pad_maximum_fusion.3), channel_id=1, source_target_pairs={{0,28},{4,0},{8,4},{12,8},{16,12},{20,16},{24,20},{28,24},{1,29},{... | collective-permute-start | bytes 1622024 | tf_op jit(solution)/shard_map/ppermute | solution.py:13
  17.7 2.6 %collective-permute-done.1 = f32[192,704]{1,0:T(8,128)S(1)} collective-permute-done((f32[192,704]{1,0:T(8,128)S(1)}, f32[192,704]{1,0:T(8,128)S(1)}, u32[]{:S(2)}, u32[]{:S(2)}) %collective-permute-start.1) | collective-permute-done | bytes 540704 | tf_op jit(solution)/shard_map/ppermute | solution.py:13
  20.3 9.7 %collective-permute-done = f32[192,704]{1,0:T(8,128)S(1)} collective-permute-done((f32[192,704]{1,0:T(8,128)S(1)}, f32[192,704]{1,0:T(8,128)S(1)}, u32[]{:S(2)}, u32[]{:S(2)}) %collective-permute-start) | collective-permute-done | bytes 540704 | tf_op jit(solution)/shard_map/ppermute | solution.py:13
  30.0 1.3 fusion.23
  31.6 0.8 fusion.11
  32.4 0.8 convolution_subtract_fusion.11
  33.2 0.7 fusion.37
  33.9 0.7 convolution_subtract_fusion.10
  34.7 0.7 fusion.36
  35.4 0.7 convolution_subtract_fusion.9
  36.1 0.7 fusion.35
  36.8 0.7 convolution_subtract_fusion.8
  37.6 0.7 fusion.34
  38.3 0.7 convolution_subtract_fusion.7
  39.0 0.7 fusion.33
  39.7 0.7 convolution_subtract_fusion.6
  40.5 0.7 fusion.32
  41.2 0.7 convolution_subtract_fusion.5
  41.9 0.7 fusion.31
  43.4 0.9 fusion.30
  45.0 0.7 fusion.29
  46.4 0.7 fusion.28
  47.9 0.7 fusion.27
  49.9 1.4 fusion.19
  51.3 1.2 fusion.10
  52.9 0.7 fusion.9
  53.6 12.1 %collective-permute-done.2 = f32[192,512]{1,0:T(8,128)S(1)} collective-permute-done((f32[192,512]{1,0:T(8,128)S(1)}, f32[192,512]{1,0:T(8,128)S(1)}, u32[]{:S(2)}, u32[]{:S(2)}) %collective-permute-start.2) | collective-permute-done | bytes 393248 | tf_op jit(solution)/shard_map/ppermute | solution.py:13
  65.8 0.8 slice_bitcast_fusion.4
  66.6 1.4 copy-done.4
  68.0 32.6 %all_gather.3 = f32[384,512]{1,0:T(8,128)S(1)} all-gather(f32[48,512]{1,0:T(8,128)S(1)} %bitcast.129), channel_id=1, replica_groups=mesh['wide'=8,'narrow'=4] {'wide'}, dimensions={0}, use_global_device_ids=true | all-gather | bytes 884736 | tf_op jit(solution)/shard_map/all_gather | solution.py:77
  100.6 1.6 %convolution_bitcast_fusion.3 = f32[192,512]{1,0:T(8,128)} fusion(f32[384,512]{1,0:T(8,128)S(1)} %all_gather.3, f32[192,384]{1,0:T(8,128)S(1)} %copy-done.11), kind=kOutput, calls=%fused_computation.19 | convolution fusion | flops 452984832 | bytes 1474560 | tf_op jit(solution)/shard_map/dot_general | solution.py:75
  102.3 1.8 %bitcast_dynamic-update-slice_fusion = f32[6,192,512]{2,1,0:T(8,128)} fusion(f32[6,192,512]{2,1,0:T(8,128)} %copy-done.4, f32[192,512]{1,0:T(8,128)} %collective-permute-done.3), kind=kLoop, calls=%fused_computation.53 | loop fusion | bytes 786432
  104.1 2.2 %slice_dynamic-update-slice_fusion = f32[6,192,512]{2,1,0:T(8,128)} fusion(f32[6,192,512]{2,1,0:T(8,128)} %bitcast_dynamic-update-slice_fusion, f32[3,192,512]{2,1,0:T(8,128)} %copy-done.1), kind=kLoop, calls=%fused_computation.30 | loop fusion | bytes 1572864
  106.2 1.8 %slice_dynamic-update-slice_fusion.1 = f32[6,192,512]{2,1,0:T(8,128)} fusion(f32[6,192,512]{2,1,0:T(8,128)} %slice_dynamic-update-slice_fusion, f32[3,192,512]{2,1,0:T(8,128)} %copy-done.1), kind=kLoop, calls=%fused_computation.47 | loop fusion | bytes 786432 | tf_op jit(solution)/shard_map/stack | solution.py:60
  108.0 4.0 %convolution_convert_fusion = bf16[6,512,192]{1,2,0:T(8,128)(2,1)S(1)} fusion(f32[6,192,512]{2,1,0:T(8,128)} %slice_dynamic-update-slice_fusion.1, f32[1,1,6,192,192]{4,3,2,1,0:T(8,128)S(1)} %copy-done.2), kind=kOutput, calls=%fused_computation.3 | convolution fusion | flops 1359544320 | bytes 4423680 | tf_op jit(solution)/shard_map/fij,fjr->fir/dot_general | solution.py:28
  112.0 3.4 %convolution_bitcast_fusion = f32[1152,512]{0,1:T(8,128)} fusion(bf16[1152,512]{1,0:T(8,128)(2,1)S(1)} %bitcast.127, bf16[1,1,1152,1152]{3,2,1,0:T(8,128)(2,1)S(1)} %copy-done), kind=kOutput, calls=%fused_computation | convolution fusion | flops 1358954496 | bytes 6193152 | tf_op jit(solution)/shard_map/dot_general | solution.py:86
  115.4 3.1 %copy.8 = f32[1152,512]{1,0:T(8,128)} copy(f32[1152,512]{0,1:T(8,128)} %convolution_bitcast_fusion) | data formatting | bytes 4718592 | tf_op jit(solution)/shard_map/dot_general | solution.py:86
  118.5 4.3 %convolution_bitcast_fusion.1 = f32[6,192,512]{2,1,0:T(8,128)S(1)} fusion(f32[6,192,512]{2,1,0:T(8,128)} %bitcast.126, f32[1,1,6,192,192]{4,3,2,1,0:T(8,128)} %param.6), kind=kOutput, calls=%fused_computation.2 | convolution fusion | flops 1358954496 | bytes 5603328 | tf_op jit(solution)/shard_map/fij,fjr->fir/dot_general | solution.py:28
  122.8 1.1 slice_bitcast_fusion.2
  124.6 1.4 collective-permute-start.4
  126.0 8.5 %all-reduce.2.cloned.1.call-done = f32[192,512]{1,0:T(8,128)} async-done(((f32[192,512]{1,0:T(8,128)}), f32[192,512]{1,0:T(8,128)}) %all-reduce.2.cloned.1.call-update) | async-done | bytes 393232 | tf_op jit(solution)/shard_map/psum | solution.py:82
  134.5 0.9 constant_dynamic-slice_fusion
  135.4 1.1 convolution_bitcast_fusion.2
  136.6 1.5 %fusion.17 = (f32[1,192,512]{2,1,0:T(8,128)S(1)}, f32[1,192,512]{2,1,0:T(8,128)S(1)}) fusion(f32[192,512]{1,0:T(8,128)} %collective-permute-done.4, f32[6,192,512]{2,1,0:T(8,128)} %copy-done.3, f32[192,512]{1,0:T(8,128)} %collective-permute-done.5), kind=kLoop, calls=%fused_computation.46 | loop fusion | flops 196608 | bytes 2359296 | tf_op jit(solution)/shard_map/stack | solution.py:91
  138.1 2.2 %fusion.1 = f32[1,1,3,192,512]{4,3,2,1,0:T(8,128)} fusion(f32[3,192,512]{2,1,0:T(8,128)S(1)} %convolution_bitcast_fusion.2, f32[3,192,192]{2,1,0:T(8,128)S(1)} %convolution_subtract_fusion, f32[1,192,512]{2,1,0:T(8,128)S(1)} %copy-done.6, f32[1,192,512]{2,1,0:T(8,128)S(1)} %get-tuple-element.6, f32[1,192,512]{2,1,0:T(8,128)S(1)} %get-tuple-element.5), kind=kOutput, calls=%fused_computation.6 | convolution fusion | flops 680361984 | bytes 3981312 | tf_op jit(solution)/shard_map/fij,fjr->fir/dot_general | solution.py:28
  (45 shorter events, 5.9 us)
Async XLA Ops:
  6.5 105.5 %copy-start = (bf16[1,1,1152,1152]{3,2,1,0:T(8,128)(2,1)S(1)}, bf16[1,1,1152,1152]{3,2,1,0:T(8,128)(2,1)}, u32[]{:S(2)}) copy-start(bf16[1,1,1152,1152]{3,2,1,0:T(8,128)(2,1)} %param.7) | copy-start | bytes 7962628
  6.5 128.0 %all-reduce.2.cloned.1.call-start = ((), (), s32[]{:S(2)}) async-start(), calls=%async_computation | async-start | bytes 786432 | tf_op jit(solution)/shard_map/psum | solution.py:82
  10.4 9.9 %collective-permute-start.1 = (f32[192,704]{1,0:T(8,128)S(1)}, f32[192,704]{1,0:T(8,128)S(1)}, u32[]{:S(2)}, u32[]{:S(2)}) collective-permute-start(f32[192,704]{1,0:T(8,128)S(1)} %pad_maximum_fusion.4), channel_id=1, source_target_pairs={{0,3},{1,0},{2,1},{3,2},{4,7},{5,4},{6,5},{7,6},{8,11},{9,8},{10,9... | collective-permute-start | bytes 1622024 | tf_op jit(solution)/shard_map/ppermute | solution.py:13
  13.1 16.9 %collective-permute-start = (f32[192,704]{1,0:T(8,128)S(1)}, f32[192,704]{1,0:T(8,128)S(1)}, u32[]{:S(2)}, u32[]{:S(2)}) collective-permute-start(f32[192,704]{1,0:T(8,128)S(1)} %pad_maximum_fusion.3), channel_id=1, source_target_pairs={{0,28},{4,0},{8,4},{12,8},{16,12},{20,16},{24,20},{28,24},{1,29},{... | collective-permute-start | bytes 1622024 | tf_op jit(solution)/shard_map/ppermute | solution.py:13
  20.3 9.7 %copy-start.7 = (f32[192,704]{1,0:T(8,128)}, f32[192,704]{1,0:T(8,128)S(1)}, u32[]{:S(2)}) copy-start(f32[192,704]{1,0:T(8,128)S(1)} %collective-permute-done.1) | copy-start | bytes 1622020
  30.0 1.3 copy-start.9
  48.6 1.1 copy-start.8
  48.6 1.2 copy-start.10
  49.9 1.4 copy-start.5
  51.3 1.6 %copy-start.12 = (f32[3,192,16]{1,2,0:T(8,128)S(1)}, f32[3,192,16]{1,2,0:T(8,128)}, u32[]{:S(2)}) copy-start(f32[3,192,16]{1,2,0:T(8,128)} %param.8) | copy-start | bytes 110596
  52.5 13.3 %copy-start.1 = (f32[3,192,512]{2,1,0:T(8,128)}, f32[3,192,512]{2,1,0:T(8,128)S(1)}, u32[]{:S(2)}) copy-start(f32[3,192,512]{2,1,0:T(8,128)S(1)} %fusion.10) | copy-start | bytes 3538948
  52.5 13.2 %collective-permute-start.2 = (f32[192,512]{1,0:T(8,128)S(1)}, f32[192,512]{1,0:T(8,128)S(1)}, u32[]{:S(2)}, u32[]{:S(2)}) collective-permute-start(f32[192,512]{1,0:T(8,128)S(1)} %slice_bitcast_fusion.7), channel_id=1, source_target_pairs={{0,4},{4,8},{8,12},{12,16},{16,20},{20,24},{24,28},{28,0},{1,5},{5... | collective-permute-start | bytes 1179656 | tf_op jit(solution)/shard_map/ppermute | solution.py:13
  65.8 34.8 %copy-start.11 = (f32[192,384]{1,0:T(8,128)S(1)}, f32[192,384]{1,0:T(8,128)}, u32[]{:S(2)}) copy-start(f32[192,384]{1,0:T(8,128)} %param.9) | copy-start | bytes 884740
  66.6 1.4 copy-start.4
  68.0 34.2 %collective-permute-start.3 = (f32[192,512]{1,0:T(8,128)}, f32[192,512]{1,0:T(8,128)}, u32[]{:S(2)}, u32[]{:S(2)}) collective-permute-start(f32[192,512]{1,0:T(8,128)} %get-tuple-element.15), channel_id=1, source_target_pairs={{0,1},{1,2},{2,3},{3,0},{4,5},{5,6},{6,7},{7,4},{8,9},{9,10},{10,1... | collective-permute-start | bytes 1179656 | tf_op jit(solution)/shard_map/ppermute | solution.py:13
  104.1 3.9 %copy-start.2 = (f32[1,1,6,192,192]{4,3,2,1,0:T(8,128)S(1)}, f32[1,1,6,192,192]{4,3,2,1,0:T(8,128)}, u32[]{:S(2)}) copy-start(f32[1,1,6,192,192]{4,3,2,1,0:T(8,128)} %param.6) | copy-start | bytes 2654212
  122.8 1.8 %copy-start.3 = (f32[6,192,512]{2,1,0:T(8,128)}, f32[6,192,512]{2,1,0:T(8,128)S(1)}, u32[]{:S(2)}) copy-start(f32[6,192,512]{2,1,0:T(8,128)S(1)} %convolution_bitcast_fusion.1) | copy-start | bytes 7077892
  124.6 11.9 %collective-permute-start.4 = (f32[192,512]{1,0:T(8,128)}, f32[192,512]{1,0:T(8,128)}, u32[]{:S(2)}, u32[]{:S(2)}) collective-permute-start(f32[192,512]{1,0:T(8,128)} %get-tuple-element.7), channel_id=1, source_target_pairs={{0,28},{4,0},{8,4},{12,8},{16,12},{20,16},{24,20},{28,24},{1,29},{... | collective-permute-start | bytes 1179656 | tf_op jit(solution)/shard_map/ppermute | solution.py:13
  126.0 10.6 %collective-permute-start.5 = (f32[192,512]{1,0:T(8,128)}, f32[192,512]{1,0:T(8,128)}, u32[]{:S(2)}, u32[]{:S(2)}) collective-permute-start(f32[192,512]{1,0:T(8,128)} %get-tuple-element.9), channel_id=1, source_target_pairs={{0,3},{1,0},{2,1},{3,2},{4,7},{5,4},{6,5},{7,6},{8,11},{9,8},{10,9... | collective-permute-start | bytes 1179656 | tf_op jit(solution)/shard_map/ppermute | solution.py:13
  136.5 1.6 %copy-start.6 = (f32[1,192,512]{2,1,0:T(8,128)S(1)}, f32[1,192,512]{2,1,0:T(8,128)}, u32[]{:S(2)}) copy-start(f32[1,192,512]{2,1,0:T(8,128)} %get-tuple-element.8) | copy-start | bytes 1179652
Sparse Core Ops, SparseCore 0:
  102.4 32.0 all-reduce.1
where the time goes:
time: 148 us; the launch traced here: 147 us
  matrix products  36.1 us (24%)
  waiting for transfers between devices  33 us (22%)
  blocking collectives  32.6 us (22%)
  between operations  13.8 us (9%)
  local copies, waits for them, and re-layouts  13.2 us (9%)
  other arithmetic  9.77 us (7%)
  starting transfers between devices  8.85 us (6%)
    all_gather x1, blocking collectives, per_device(): lax.all_gather(restricted_residual, 'wide', axis=0, tiled=True)  32.6 us
    ppermute x6, waiting for transfers between devices, passed_along(): return lax.ppermute(value, axis, pairs)  24.5 us
    dot_general x4, matrix products, apply_faces(): jnp.einsum('fij,fjr->fir', blocks, fields, precision=exact_arithmetic_mode)  11.7 us
    dot_general x12, matrix products, newton_schulz(): jnp.einsum('bij,bjk->bik', matrices, approx, precision=exact_arithmetic_m...  8.92 us
    ppermute x6, starting transfers between devices, passed_along(): return lax.ppermute(value, axis, pairs)  8.85 us
    dot_general x12, matrix products, newton_schulz(): jnp.einsum('bij,bjk->bik', approx, product, precision=exact_arithmetic_mode)  8.59 us
    psum x1, waiting for transfers between devices, per_device(): summed = lax.psum(incomplete_total, 'narrow')  8.51 us
    unnamed x29, local copies, waits for them, and re-layouts  6.61 us
  transfers between devices with their start and end apart: 7, of which 4 were waited for; matrix products, arithmetic and copies ran while one was open for 18% of the time, Pallas kernels for 0%

commit v1 on v0

--- a/solution.py
+++ b/solution.py
@@ -5,6 +5,22 @@
 
 NS_STEPS = 12
 exact_arithmetic_mode = lax.Precision.HIGHEST
+
+
+def ring_gather(x, axis, dim):
+    ways, here, step = (lax.axis_size(axis), lax.axis_index(axis), x.shape[dim])
+    lengths = [n * ways if d == dim else n for d, n in enumerate(x.shape)]
+    full = lax.dynamic_update_slice_in_dim(jnp.zeros(lengths, x.dtype), x, here * step, axis=dim)
+    going_up = going_down = x
+    for far in range(1, ways // 2 + 1):
+        going_up = lax.ppermute(going_up, axis, [(d, (d + 1) % ways) for d in range(ways)])
+        full = lax.dynamic_update_slice_in_dim(full, going_up, (here - far) % ways * step, axis=dim)
+        if 2 * far < ways:
+            going_down = lax.ppermute(going_down, axis, [(d, (d - 1) % ways) for d in range(ways)])
+            full = lax.dynamic_update_slice_in_dim(
+                full, going_down, (here + far) % ways * step, axis=dim
+            )
+    return full
 
 
 def passed_along(value, axis, steps):
@@ -74,7 +90,7 @@
     restricted_residual = restricted_residual.reshape(-1, columns_count)
     incomplete_total = jnp.dot(
         coarse_inverse,
-        lax.all_gather(restricted_residual, "wide", axis=0, tiled=True),
+        ring_gather(restricted_residual, "wide", 0),
         precision=exact_arithmetic_mode,
         preferred_element_type=jnp.float32,
     )

time: 148 us -> 141 us (0.953)
  blocking collectives: 32.6 us -> 0 us
  starting transfers between devices: 8.85 us -> 23.7 us
  waiting for transfers between devices: 33 us -> 40.1 us
  local copies, waits for them, and re-layouts: 13.2 us -> 15.4 us
    all_gather x1 -> x0, blocking collectives: 32.6 us -> none  [per_device(): lax.all_gather(restricted_residual, 'wide', axis=0, tiled=True)]
    ppermute x0 -> x7, waiting for transfers between devices: none -> 19.7 us  [the longest x4 10.2 us: ring_gather(): lax.ppermute(going_up, axis, [(d, (d + 1) % ways) for d in range(ways)])]
    ppermute x0 -> x7, starting transfers between devices: none -> 12 us  [the longest x3 9.95 us: ring_gather(): lax.ppermute(going_down, axis, [(d, (d - 1) % ways) for d in range(ways)])]
    ppermute x6, waiting for transfers between devices: 24.5 us -> 17.2 us  [passed_along(): return lax.ppermute(value, axis, pairs)]
    psum x1, waiting for transfers between devices: 8.51 us -> 3.15 us  [per_device(): summed = lax.psum(incomplete_total, 'narrow')]
    ppermute x6, starting transfers between devices: 8.85 us -> 11.7 us  [passed_along(): return lax.ppermute(value, axis, pairs)]
    dynamic_update_slice x0 -> x8, local copies, waits for them, and re-layouts: none -> 1.99 us  [the longest x1 1.01 us: ring_gather(): lax.dynamic_update_slice_in_dim(jnp.zeros(lengths, x.dtype), x, here * st...]
    unnamed x29 -> x33, local copies, waits for them, and re-layouts: 6.61 us -> 6.75 us
  transfers between devices with their start and end apart: 7 -> 14, of which waited for: 4 -> 8; matrix products, arithmetic and copies ran while one was open for 18% -> 35% of each run, Pallas kernels for 0% -> 0%
where the time goes in v1:
time: 141 us; the launch traced here: 140 us
  waiting for transfers between devices  40.1 us (28%)
  matrix products  36.7 us (26%)
  starting transfers between devices  23.7 us (17%)
  local copies, waits for them, and re-layouts  15.4 us (11%)
  between operations  13.9 us (10%)
  other arithmetic  10.7 us (8%)
    ppermute x6, waiting for transfers between devices, passed_along(): return lax.ppermute(value, axis, pairs)  17.2 us
    ppermute x6, starting transfers between devices, passed_along(): return lax.ppermute(value, axis, pairs)  11.7 us
    dot_general x4, matrix products, apply_faces(): jnp.einsum('fij,fjr->fir', blocks, fields, precision=exact_arithmetic_mode)  11.7 us
    ppermute x4, waiting for transfers between devices, ring_gather(): lax.ppermute(going_up, axis, [(d, (d + 1) % ways) for d in range(ways)])  10.2 us
    ppermute x3, starting transfers between devices, ring_gather(): lax.ppermute(going_down, axis, [(d, (d - 1) % ways) for d in range(ways)])  9.95 us
    ppermute x3, waiting for transfers between devices, ring_gather(): lax.ppermute(going_down, axis, [(d, (d - 1) % ways) for d in range(ways)])  9.46 us
    dot_general x12, matrix products, newton_schulz(): jnp.einsum('bij,bjk->bik', matrices, approx, precision=exact_arithmetic_m...  8.94 us
    dot_general x12, matrix products, newton_schulz(): jnp.einsum('bij,bjk->bik', approx, product, precision=exact_arithmetic_mode)  8.57 us
  transfers between devices with their start and end apart: 14, of which 8 were waited for; matrix products, arithmetic and copies ran while one was open for 35% of the time, Pallas kernels for 0%

profile of v1, /device:TPU:0, one launch (start us, length us, event | category | flops | bytes accessed | tf_op | source)
XLA Modules:
  0.0 140.5 jit_solution(12704866786178853494)
XLA Ops:
  6.5 1.4 %add_bitcast_fusion.1 = (f32[1,192,192]{2,1,0:T(8,128)S(1)}, f32[192,192]{1,0:T(8,128)S(1)}, f32[192,192]{1,0:T(8,128)S(1)}) fusion(f32[1,1,6,192,192]{4,3,2,1,0:T(8,128)} %param.6), kind=kLoop, calls=%fused_computation.66 | loop fusion | flops 36864 | bytes 1032192 | tf_op jit(solution)/shard_map/add | solution.py:60
  8.0 1.5 %slice_bitcast_fusion.6 = (f32[192,512]{1,0:T(8,128)S(1)}, f32[192,512]{1,0:T(8,128)S(1)}, f32[1,192,512]{2,1,0:T(8,128)S(1)}) fusion(f32[1,1,6,192,512]{4,3,2,1,0:T(8,128)} %param.5), kind=kLoop, calls=%fused_computation.57 | loop fusion | flops 98304 | bytes 2752512 | tf_op jit(solution)/shard_map/squeeze | solution.py:52
  9.5 1.0 pad_maximum_fusion.4
  10.5 2.4 %collective-permute-start.1 = (f32[192,704]{1,0:T(8,128)}, f32[192,704]{1,0:T(8,128)}, u32[]{:S(2)}, u32[]{:S(2)}) collective-permute-start(f32[192,704]{1,0:T(8,128)} %pad_maximum_fusion.4), channel_id=1, source_target_pairs={{0,3},{1,0},{2,1},{3,2},{4,7},{5,4},{6,5},{7,6},{8,11},{9,8},{10,9... | collective-permute-start | bytes 1622024 | tf_op jit(solution)/shard_map/ppermute | solution.py:29
  12.9 1.0 pad_maximum_fusion.3
  13.9 4.6 %collective-permute-start = (f32[192,704]{1,0:T(8,128)}, f32[192,704]{1,0:T(8,128)}, u32[]{:S(2)}, u32[]{:S(2)}) collective-permute-start(f32[192,704]{1,0:T(8,128)} %pad_maximum_fusion.3), channel_id=1, source_target_pairs={{0,28},{4,0},{8,4},{12,8},{16,12},{20,16},{24,20},{28,24},{1,29},{... | collective-permute-start | bytes 1622024 | tf_op jit(solution)/shard_map/ppermute | solution.py:29
  18.4 2.1 %collective-permute-done.1 = f32[192,704]{1,0:T(8,128)} collective-permute-done((f32[192,704]{1,0:T(8,128)}, f32[192,704]{1,0:T(8,128)}, u32[]{:S(2)}, u32[]{:S(2)}) %collective-permute-start.1) | collective-permute-done | bytes 540704 | tf_op jit(solution)/shard_map/ppermute | solution.py:29
  20.6 10.5 %collective-permute-done = f32[192,704]{1,0:T(8,128)} collective-permute-done((f32[192,704]{1,0:T(8,128)}, f32[192,704]{1,0:T(8,128)}, u32[]{:S(2)}, u32[]{:S(2)}) %collective-permute-start) | collective-permute-done | bytes 540704 | tf_op jit(solution)/shard_map/ppermute | solution.py:29
  31.1 1.7 %fusion.19 = (f32[1,192,512]{2,1,0:T(8,128)S(1)}, f32[1,192,512]{2,1,0:T(8,128)S(1)}) fusion(f32[192,704]{1,0:T(8,128)} %collective-permute-done, f32[1,1,6,192,512]{4,3,2,1,0:T(8,128)} %param.5, f32[192,704]{1,0:T(8,128)} %collective-permute-done.1), kind=kLoop, calls=%fused_computation.52 | loop fusion | flops 196608 | bytes 2359296 | tf_op jit(solution)/shard_map/stack | solution.py:64
  32.8 1.4 fusion.9
  34.2 5.2 %collective-permute-start.7 = (f32[48,512]{1,0:T(8,128)}, f32[48,512]{1,0:T(8,128)}, u32[]{:S(2)}, u32[]{:S(2)}) collective-permute-start(f32[48,512]{1,0:T(8,128)} %bitcast.32), channel_id=1, source_target_pairs={{0,28},{4,0},{8,4},{12,8},{16,12},{20,16},{24,20},{28,24},{1,29},{... | collective-permute-start | bytes 294920 | tf_op jit(solution)/shard_map/ppermute | solution.py:19
  39.4 1.3 fusion.23
  41.0 0.8 fusion.11
  41.8 0.8 convolution_subtract_fusion.11
  45.5 0.7 fusion.35
  46.9 0.7 fusion.34
  48.4 0.7 fusion.33
  49.8 0.7 fusion.32
  51.3 0.7 fusion.31
  52.7 0.9 fusion.30
  59.2 1.2 fusion.10
  60.6 1.0 constant_dynamic-update-slice_fusion.7
  61.6 4.8 %collective-permute-start.9 = (f32[48,512]{1,0:T(8,128)}, f32[48,512]{1,0:T(8,128)S(1)}, u32[]{:S(2)}, u32[]{:S(2)}) collective-permute-start(f32[48,512]{1,0:T(8,128)} %collective-permute-done.7), channel_id=1, source_target_pairs={{0,28},{4,0},{8,4},{12,8},{16,12},{20,16},{24,20},{28,24},{1,29},{... | collective-permute-start | bytes 294920 | tf_op jit(solution)/shard_map/ppermute | solution.py:19
  66.4 0.9 constant_dynamic-update-slice_fusion.5
  67.3 9.5 %collective-permute-done.9 = f32[48,512]{1,0:T(8,128)S(1)} collective-permute-done((f32[48,512]{1,0:T(8,128)}, f32[48,512]{1,0:T(8,128)S(1)}, u32[]{:S(2)}, u32[]{:S(2)}) %collective-permute-start.9) | collective-permute-done | bytes 98336 | tf_op jit(solution)/shard_map/ppermute | solution.py:19
  76.8 2.0 %collective-permute-start.10 = (f32[48,512]{1,0:T(8,128)S(1)}, f32[48,512]{1,0:T(8,128)S(1)}, u32[]{:S(2)}, u32[]{:S(2)}) collective-permute-start(f32[48,512]{1,0:T(8,128)S(1)} %collective-permute-done.8), channel_id=1, source_target_pairs={{0,4},{4,8},{8,12},{12,16},{16,20},{20,24},{24,28},{28,0},{1,5},{5... | collective-permute-start | bytes 294920 | tf_op jit(solution)/shard_map/ppermute | solution.py:16
  78.8 5.3 %collective-permute-done.10 = f32[48,512]{1,0:T(8,128)S(1)} collective-permute-done((f32[48,512]{1,0:T(8,128)S(1)}, f32[48,512]{1,0:T(8,128)S(1)}, u32[]{:S(2)}, u32[]{:S(2)}) %collective-permute-start.10) | collective-permute-done | bytes 98336 | tf_op jit(solution)/shard_map/ppermute | solution.py:16
  84.2 0.8 slice_bitcast_fusion.4
  85.0 1.4 %copy-done.4 = f32[6,192,512]{2,1,0:T(8,128)} copy-done((f32[6,192,512]{2,1,0:T(8,128)}, f32[6,192,512]{2,1,0:T(8,128)S(1)}, u32[]{:S(2)}) %copy-start.4) | copy-done | bytes 2359320
  86.4 5.0 %collective-permute-done.12 = f32[48,512]{1,0:T(8,128)S(1)} collective-permute-done((f32[48,512]{1,0:T(8,128)S(1)}, f32[48,512]{1,0:T(8,128)S(1)}, u32[]{:S(2)}, u32[]{:S(2)}) %collective-permute-start.12) | collective-permute-done | bytes 98336 | tf_op jit(solution)/shard_map/ppermute | solution.py:16
  91.4 1.6 %convolution_bitcast_fusion.3 = f32[192,512]{1,0:T(8,128)} fusion(f32[384,512]{1,0:T(8,128)S(1)} %constant_dynamic-update-slice_fusion, f32[192,384]{1,0:T(8,128)S(1)} %copy-done.12), kind=kOutput, calls=%fused_computation.19 | convolution fusion | flops 452984832 | bytes 1474560 | tf_op jit(solution)/shard_map/dot_general | solution.py:91
  93.1 0.9 collective-permute-done.3
  93.9 1.8 %bitcast_dynamic-update-slice_fusion = f32[6,192,512]{2,1,0:T(8,128)} fusion(f32[6,192,512]{2,1,0:T(8,128)} %copy-done.4, f32[192,512]{1,0:T(8,128)} %collective-permute-done.3), kind=kLoop, calls=%fused_computation.53 | loop fusion | bytes 786432
  95.7 2.2 %slice_dynamic-update-slice_fusion = f32[6,192,512]{2,1,0:T(8,128)} fusion(f32[6,192,512]{2,1,0:T(8,128)} %bitcast_dynamic-update-slice_fusion, f32[3,192,512]{2,1,0:T(8,128)} %copy-done.1), kind=kLoop, calls=%fused_computation.30 | loop fusion | bytes 1572864
  97.9 1.8 %slice_dynamic-update-slice_fusion.1 = f32[6,192,512]{2,1,0:T(8,128)} fusion(f32[6,192,512]{2,1,0:T(8,128)} %slice_dynamic-update-slice_fusion, f32[3,192,512]{2,1,0:T(8,128)} %copy-done.1), kind=kLoop, calls=%fused_computation.47 | loop fusion | bytes 786432 | tf_op jit(solution)/shard_map/stack | solution.py:76
  99.7 4.0 %convolution_convert_fusion = bf16[6,512,192]{1,2,0:T(8,128)(2,1)S(1)} fusion(f32[6,192,512]{2,1,0:T(8,128)} %slice_dynamic-update-slice_fusion.1, f32[1,1,6,192,192]{4,3,2,1,0:T(8,128)S(1)} %copy-done.2), kind=kOutput, calls=%fused_computation.3 | convolution fusion | flops 1359544320 | bytes 4423680 | tf_op jit(solution)/shard_map/fij,fjr->fir/dot_general | solution.py:44
  103.7 3.4 %convolution_bitcast_fusion = f32[1152,512]{0,1:T(8,128)} fusion(bf16[1152,512]{1,0:T(8,128)(2,1)S(1)} %bitcast.127, bf16[1,1,1152,1152]{3,2,1,0:T(8,128)(2,1)S(1)} %copy-done), kind=kOutput, calls=%fused_computation | convolution fusion | flops 1358954496 | bytes 6193152 | tf_op jit(solution)/shard_map/dot_general | solution.py:102
  107.1 3.1 %copy.8 = f32[1152,512]{1,0:T(8,128)} copy(f32[1152,512]{0,1:T(8,128)} %convolution_bitcast_fusion) | data formatting | bytes 4718592 | tf_op jit(solution)/shard_map/dot_general | solution.py:102
  110.2 4.3 %convolution_bitcast_fusion.1 = f32[6,192,512]{2,1,0:T(8,128)S(1)} fusion(f32[6,192,512]{2,1,0:T(8,128)} %bitcast.126, f32[1,1,6,192,192]{4,3,2,1,0:T(8,128)} %param.6), kind=kOutput, calls=%fused_computation.2 | convolution fusion | flops 1358954496 | bytes 5603328 | tf_op jit(solution)/shard_map/fij,fjr->fir/dot_general | solution.py:44
  114.5 1.1 slice_bitcast_fusion.2
  115.6 0.7 copy-done.3
  116.3 4.7 %collective-permute-start.4 = (f32[192,512]{1,0:T(8,128)}, f32[192,512]{1,0:T(8,128)}, u32[]{:S(2)}, u32[]{:S(2)}) collective-permute-start(f32[192,512]{1,0:T(8,128)} %get-tuple-element.7), channel_id=1, source_target_pairs={{0,28},{4,0},{8,4},{12,8},{16,12},{20,16},{24,20},{28,24},{1,29},{... | collective-permute-start | bytes 1179656 | tf_op jit(solution)/shard_map/ppermute | solution.py:29
  121.0 3.1 %all-reduce.2.cloned.1.call-done = f32[192,512]{1,0:T(8,128)} async-done(((f32[192,512]{1,0:T(8,128)}), f32[192,512]{1,0:T(8,128)}) %all-reduce.2.cloned.1.call-update) | async-done | bytes 393232 | tf_op jit(solution)/shard_map/psum | solution.py:98
  124.2 0.9 constant_dynamic-slice_fusion
  125.1 1.1 convolution_bitcast_fusion.2
  126.2 3.7 %collective-permute-done.4 = f32[192,512]{1,0:T(8,128)} collective-permute-done((f32[192,512]{1,0:T(8,128)}, f32[192,512]{1,0:T(8,128)}, u32[]{:S(2)}, u32[]{:S(2)}) %collective-permute-start.4) | collective-permute-done | bytes 393248 | tf_op jit(solution)/shard_map/ppermute | solution.py:29
  129.9 1.5 %fusion.17 = (f32[1,192,512]{2,1,0:T(8,128)S(1)}, f32[1,192,512]{2,1,0:T(8,128)S(1)}) fusion(f32[192,512]{1,0:T(8,128)} %collective-permute-done.4, f32[6,192,512]{2,1,0:T(8,128)} %copy-done.3, f32[192,512]{1,0:T(8,128)} %collective-permute-done.5), kind=kLoop, calls=%fused_computation.46 | loop fusion | flops 196608 | bytes 2359296 | tf_op jit(solution)/shard_map/stack | solution.py:107
  131.4 2.2 %fusion.1 = f32[1,1,3,192,512]{4,3,2,1,0:T(8,128)} fusion(f32[3,192,512]{2,1,0:T(8,128)S(1)} %convolution_bitcast_fusion.2, f32[3,192,192]{2,1,0:T(8,128)S(1)} %convolution_subtract_fusion, f32[1,192,512]{2,1,0:T(8,128)S(1)} %copy-done.11, f32[1,192,512]{2,1,0:T(8,128)S(1)} %get-tuple-element.6, f32[1,192,512]{2,1,0:T(8,128)S(1)} %get-tuple-element.5), kind=kOutput, calls=%fused_computation.6 | convolution fusion | flops 680361984 | bytes 3981312 | tf_op jit(solution)/shard_map/fij,fjr->fir/dot_general | solution.py:44
  (71 shorter events, 12.6 us)
Async XLA Ops:
  6.5 97.1 %copy-start = (bf16[1,1,1152,1152]{3,2,1,0:T(8,128)(2,1)S(1)}, bf16[1,1,1152,1152]{3,2,1,0:T(8,128)(2,1)}, u32[]{:S(2)}) copy-start(bf16[1,1,1152,1152]{3,2,1,0:T(8,128)(2,1)} %param.7) | copy-start | bytes 7962628
  6.5 117.6 %all-reduce.2.cloned.1.call-start = ((), (), s32[]{:S(2)}) async-start(), calls=%async_computation | async-start | bytes 786432 | tf_op jit(solution)/shard_map/psum | solution.py:98
  9.5 23.4 %copy-start.9 = (f32[1,192,512]{2,1,0:T(8,128)}, f32[1,192,512]{2,1,0:T(8,128)S(1)}, u32[]{:S(2)}) copy-start(f32[1,192,512]{2,1,0:T(8,128)S(1)} %get-tuple-element.14) | copy-start | bytes 1179652
  10.5 10.1 %collective-permute-start.1 = (f32[192,704]{1,0:T(8,128)}, f32[192,704]{1,0:T(8,128)}, u32[]{:S(2)}, u32[]{:S(2)}) collective-permute-start(f32[192,704]{1,0:T(8,128)} %pad_maximum_fusion.4), channel_id=1, source_target_pairs={{0,3},{1,0},{2,1},{3,2},{4,7},{5,4},{6,5},{7,6},{8,11},{9,8},{10,9... | collective-permute-start | bytes 1622024 | tf_op jit(solution)/shard_map/ppermute | solution.py:29
  13.9 17.2 %collective-permute-start = (f32[192,704]{1,0:T(8,128)}, f32[192,704]{1,0:T(8,128)}, u32[]{:S(2)}, u32[]{:S(2)}) collective-permute-start(f32[192,704]{1,0:T(8,128)} %pad_maximum_fusion.3), channel_id=1, source_target_pairs={{0,28},{4,0},{8,4},{12,8},{16,12},{20,16},{24,20},{28,24},{1,29},{... | collective-permute-start | bytes 1622024 | tf_op jit(solution)/shard_map/ppermute | solution.py:29
  18.4 14.4 %copy-start.13 = (f32[3,192,16]{1,2,0:T(8,128)S(1)}, f32[3,192,16]{1,2,0:T(8,128)}, u32[]{:S(2)}) copy-start(f32[3,192,16]{1,2,0:T(8,128)} %param.8) | copy-start | bytes 110596
  32.8 7.9 %copy-start.5 = (f32[1,192,512]{2,1,0:T(8,128)}, f32[1,192,512]{2,1,0:T(8,128)S(1)}, u32[]{:S(2)}) copy-start(f32[1,192,512]{2,1,0:T(8,128)S(1)} %get-tuple-element.10) | copy-start | bytes 1179652
  32.8 7.9 %copy-start.7 = (f32[1,192,512]{2,1,0:T(8,128)}, f32[1,192,512]{2,1,0:T(8,128)S(1)}, u32[]{:S(2)}) copy-start(f32[1,192,512]{2,1,0:T(8,128)S(1)} %get-tuple-element.11) | copy-start | bytes 1179652
  34.2 27.4 %collective-permute-start.7 = (f32[48,512]{1,0:T(8,128)}, f32[48,512]{1,0:T(8,128)}, u32[]{:S(2)}, u32[]{:S(2)}) collective-permute-start(f32[48,512]{1,0:T(8,128)} %bitcast.32), channel_id=1, source_target_pairs={{0,28},{4,0},{8,4},{12,8},{16,12},{20,16},{24,20},{28,24},{1,29},{... | collective-permute-start | bytes 294920 | tf_op jit(solution)/shard_map/ppermute | solution.py:19
  39.4 27.0 %collective-permute-start.6 = (f32[48,512]{1,0:T(8,128)}, f32[48,512]{1,0:T(8,128)S(1)}, u32[]{:S(2)}, u32[]{:S(2)}) collective-permute-start(f32[48,512]{1,0:T(8,128)} %bitcast.32), channel_id=1, source_target_pairs={{0,4},{4,8},{8,12},{12,16},{16,20},{20,24},{24,28},{28,0},{1,5},{5... | collective-permute-start | bytes 294920 | tf_op jit(solution)/shard_map/ppermute | solution.py:16
  58.0 1.0 copy-start.6
  58.0 1.1 copy-start.8
  58.0 1.2 copy-start.10
  60.4 23.8 %copy-start.1 = (f32[3,192,512]{2,1,0:T(8,128)}, f32[3,192,512]{2,1,0:T(8,128)S(1)}, u32[]{:S(2)}) copy-start(f32[3,192,512]{2,1,0:T(8,128)S(1)} %fusion.10) | copy-start | bytes 3538948
  60.4 23.7 %collective-permute-start.2 = (f32[192,512]{1,0:T(8,128)S(1)}, f32[192,512]{1,0:T(8,128)S(1)}, u32[]{:S(2)}, u32[]{:S(2)}) collective-permute-start(f32[192,512]{1,0:T(8,128)S(1)} %slice_bitcast_fusion.7), channel_id=1, source_target_pairs={{0,4},{4,8},{8,12},{12,16},{16,20},{20,24},{24,28},{28,0},{1,5},{5... | collective-permute-start | bytes 1179656 | tf_op jit(solution)/shard_map/ppermute | solution.py:29
  61.6 15.2 %collective-permute-start.9 = (f32[48,512]{1,0:T(8,128)}, f32[48,512]{1,0:T(8,128)S(1)}, u32[]{:S(2)}, u32[]{:S(2)}) collective-permute-start(f32[48,512]{1,0:T(8,128)} %collective-permute-done.7), channel_id=1, source_target_pairs={{0,28},{4,0},{8,4},{12,8},{16,12},{20,16},{24,20},{28,24},{1,29},{... | collective-permute-start | bytes 294920 | tf_op jit(solution)/shard_map/ppermute | solution.py:19
  66.4 10.4 %collective-permute-start.8 = (f32[48,512]{1,0:T(8,128)S(1)}, f32[48,512]{1,0:T(8,128)S(1)}, u32[]{:S(2)}, u32[]{:S(2)}) collective-permute-start(f32[48,512]{1,0:T(8,128)S(1)} %collective-permute-done.6), channel_id=1, source_target_pairs={{0,4},{4,8},{8,12},{12,16},{16,20},{20,24},{24,28},{28,0},{1,5},{5... | collective-permute-start | bytes 294920 | tf_op jit(solution)/shard_map/ppermute | solution.py:16
  76.8 9.6 %collective-permute-start.11 = (f32[48,512]{1,0:T(8,128)S(1)}, f32[48,512]{1,0:T(8,128)S(1)}, u32[]{:S(2)}, u32[]{:S(2)}) collective-permute-start(f32[48,512]{1,0:T(8,128)S(1)} %collective-permute-done.9), channel_id=1, source_target_pairs={{0,28},{4,0},{8,4},{12,8},{16,12},{20,16},{24,20},{28,24},{1,29},{... | collective-permute-start | bytes 294920 | tf_op jit(solution)/shard_map/ppermute | solution.py:19
  76.8 7.3 %collective-permute-start.10 = (f32[48,512]{1,0:T(8,128)S(1)}, f32[48,512]{1,0:T(8,128)S(1)}, u32[]{:S(2)}, u32[]{:S(2)}) collective-permute-start(f32[48,512]{1,0:T(8,128)S(1)} %collective-permute-done.8), channel_id=1, source_target_pairs={{0,4},{4,8},{8,12},{12,16},{16,20},{20,24},{24,28},{28,0},{1,5},{5... | collective-permute-start | bytes 294920 | tf_op jit(solution)/shard_map/ppermute | solution.py:16
  84.1 7.3 %collective-permute-start.12 = (f32[48,512]{1,0:T(8,128)S(1)}, f32[48,512]{1,0:T(8,128)S(1)}, u32[]{:S(2)}, u32[]{:S(2)}) collective-permute-start(f32[48,512]{1,0:T(8,128)S(1)} %collective-permute-done.10), channel_id=1, source_target_pairs={{0,4},{4,8},{8,12},{12,16},{16,20},{20,24},{24,28},{28,0},{1,5},{5... | collective-permute-start | bytes 294920 | tf_op jit(solution)/shard_map/ppermute | solution.py:16
  84.1 7.3 %copy-start.12 = (f32[192,384]{1,0:T(8,128)S(1)}, f32[192,384]{1,0:T(8,128)}, u32[]{:S(2)}) copy-start(f32[192,384]{1,0:T(8,128)} %param.9) | copy-start | bytes 884740
  85.0 1.4 %copy-start.4 = (f32[6,192,512]{2,1,0:T(8,128)}, f32[6,192,512]{2,1,0:T(8,128)S(1)}, u32[]{:S(2)}) copy-start(f32[6,192,512]{2,1,0:T(8,128)S(1)} %get-tuple-element.16) | copy-start | bytes 7077892
  86.4 7.5 %collective-permute-start.3 = (f32[192,512]{1,0:T(8,128)}, f32[192,512]{1,0:T(8,128)}, u32[]{:S(2)}, u32[]{:S(2)}) collective-permute-start(f32[192,512]{1,0:T(8,128)} %get-tuple-element.15), channel_id=1, source_target_pairs={{0,1},{1,2},{2,3},{3,0},{4,5},{5,6},{6,7},{7,4},{8,9},{9,10},{10,1... | collective-permute-start | bytes 1179656 | tf_op jit(solution)/shard_map/ppermute | solution.py:29
  95.7 4.0 %copy-start.2 = (f32[1,1,6,192,192]{4,3,2,1,0:T(8,128)S(1)}, f32[1,1,6,192,192]{4,3,2,1,0:T(8,128)}, u32[]{:S(2)}) copy-start(f32[1,1,6,192,192]{4,3,2,1,0:T(8,128)} %param.6) | copy-start | bytes 2654212
  114.5 1.8 %copy-start.3 = (f32[6,192,512]{2,1,0:T(8,128)}, f32[6,192,512]{2,1,0:T(8,128)S(1)}, u32[]{:S(2)}) copy-start(f32[6,192,512]{2,1,0:T(8,128)S(1)} %convolution_bitcast_fusion.1) | copy-start | bytes 7077892
  114.5 10.6 %copy-start.14 = (f32[3,192,16]{1,2,0:T(8,128)S(1)}, f32[3,192,16]{1,2,0:T(8,128)}, u32[]{:S(2)}) copy-start(f32[3,192,16]{1,2,0:T(8,128)} %param.8) | copy-start | bytes 110596
  116.3 13.6 %collective-permute-start.4 = (f32[192,512]{1,0:T(8,128)}, f32[192,512]{1,0:T(8,128)}, u32[]{:S(2)}, u32[]{:S(2)}) collective-permute-start(f32[192,512]{1,0:T(8,128)} %get-tuple-element.7), channel_id=1, source_target_pairs={{0,28},{4,0},{8,4},{12,8},{16,12},{20,16},{24,20},{28,24},{1,29},{... | collective-permute-start | bytes 1179656 | tf_op jit(solution)/shard_map/ppermute | solution.py:29
  121.0 8.9 %collective-permute-start.5 = (f32[192,512]{1,0:T(8,128)}, f32[192,512]{1,0:T(8,128)}, u32[]{:S(2)}, u32[]{:S(2)}) collective-permute-start(f32[192,512]{1,0:T(8,128)} %get-tuple-element.9), channel_id=1, source_target_pairs={{0,3},{1,0},{2,1},{3,2},{4,7},{5,4},{6,5},{7,6},{8,11},{9,8},{10,9... | collective-permute-start | bytes 1179656 | tf_op jit(solution)/shard_map/ppermute | solution.py:29
  126.2 5.2 %copy-start.11 = (f32[1,192,512]{2,1,0:T(8,128)S(1)}, f32[1,192,512]{2,1,0:T(8,128)}, u32[]{:S(2)}) copy-start(f32[1,192,512]{2,1,0:T(8,128)} %get-tuple-element.8) | copy-start | bytes 1179652
Sparse Core Ops, SparseCore 0:
  93.2 30.9 all-reduce.1
